TPU v7x, 32 devices: a whole 2x2x4 slice. The times are simulated.
32 devices in a mesh: rep: 2 (over x), shard: 16 (over z, y, core).
Axes of the slice: x: 2, y: 2, z: 4, core: 2. Of those that a mesh axis runs over, the one named last changes fastest.
Arguments:
- tokens: bfloat16 [2, 32, 64, 1024], P(None, ('rep', 'shard')), may hold values from -6 to 6
- prefix: int32 [2, 32], P(None, ('rep', 'shard')), may hold values from 6 to 32
- qkv_weight: bfloat16 [1024, 3072], P('shard'), may hold values from -0.1875 to 0.1875
- out_weight: bfloat16 [1024, 1024], P('shard'), may hold values from -1 to 1
- in_weight: bfloat16 [1024, 5632], P('shard'), may hold values from -0.1875 to 0.1875
- down_weight: bfloat16 [2816, 1024], P('shard'), may hold values from -0.109375 to 0.109375
- cotangent: bfloat16 [2, 32, 64, 1024], P(None, ('rep', 'shard')), may hold values from -6 to 6
Outputs:
- result: bfloat16 [2, 32, 64, 1024], P(None, ('rep', 'shard'))
- grad_tokens: float32 [2, 32, 64, 1024], P(None, ('rep', 'shard'))
- grad_qkv: float32 [1024, 3072], P('shard')
- grad_out: float32 [1024, 1024], P('shard')
- grad_in: float32 [1024, 5632], P('shard')
- grad_down: float32 [2816, 1024], P('shard')
Inputs may be any that keep to these rules, and one draw needn't show every extreme that they name: Each sequence's prefix length, a tenth to a half of 64.
All inputs are finite; a program needn't handle non-finite values.
Results may differ from a plain program's by a relative error of at most 0.014.
Values may be sent and summed in bfloat16 or wider, within the bound.
No kernel may reach another device: no remote copies, remote signals or barrier semaphores. Data moves between devices by JAX's collectives and lax.ppermute only.
A program may use at most 256 MiB of HBM per device.

v0:
```python
import jax
import jax.numpy as jnp
from jax import lax
from jax.sharding import PartitionSpec as P

H = 16
HD = 64


def norm_rows(values):
    centre = values - jnp.mean(values, axis=-1, keepdims=True)
    inverse = lax.rsqrt(jnp.mean(centre * centre, axis=-1, keepdims=True) + 1e-05)
    return (centre * inverse, inverse)


def norm_back(normed, inverse, upstream):
    return inverse * (
        upstream
        - jnp.mean(upstream, axis=-1, keepdims=True)
        - normed * jnp.mean(upstream * normed, axis=-1, keepdims=True)
    )


def rope_tables(length, head_size):
    position = jnp.arange(length, dtype=jnp.float32)[:, None]
    frequency = 10000.0 ** (-jnp.arange(0, head_size, 2, dtype=jnp.float32) / head_size)
    angles = position * frequency[None, :]
    angles = jnp.concatenate([angles, angles], axis=-1)
    return (jnp.cos(angles)[:, None, :], jnp.sin(angles)[:, None, :])


def rotate(values, cosine, sine):
    half_size = values.shape[-1] // 2
    turned = jnp.concatenate([-values[..., half_size:], values[..., :half_size]], axis=-1)
    return values * cosine + turned * sine


def rotate_back(grads, cosine, sine):
    half_size = grads.shape[-1] // 2
    scaled = grads * sine
    return grads * cosine + jnp.concatenate(
        [scaled[..., half_size:], -scaled[..., :half_size]], axis=-1
    )


def transpose_dot(left, right):
    return lax.dot_general(
        left, right, (((1,), (1,)), ((), ())), preferred_element_type=jnp.float32
    )


def inner_rows(left, right):
    return lax.dot_general(
        left, right, (((0,), (0,)), ((), ())), preferred_element_type=jnp.float32
    )


def masked_scores(query, keys, allowed, scale):
    scores = jnp.einsum("lhe,mhe->hlm", query, keys, preferred_element_type=jnp.float32) * scale
    return jnp.where(allowed[None], scores, -1e30)


def attend(query, keys, values, allowed, scale):
    scores = masked_scores(query, keys, allowed, scale)
    highest = jnp.max(scores, axis=-1, keepdims=True)
    expo = jnp.exp(scores - highest)
    summed = jnp.sum(expo, axis=-1, keepdims=True)
    probs = (expo / summed).astype(jnp.bfloat16)
    output = jnp.einsum("hlm,mhe->lhe", probs, values, preferred_element_type=jnp.float32)
    return (output, highest + jnp.log(summed))


def attend_back(query, keys, values, log_total, grad_out, allowed, scale):
    probs = jnp.exp(masked_scores(query, keys, allowed, scale) - log_total)
    dprob = jnp.einsum("lhe,mhe->hlm", grad_out, values, preferred_element_type=jnp.float32)
    centre = jnp.sum(probs * dprob, axis=-1, keepdims=True)
    dscore = (probs * (dprob - centre)).astype(jnp.bfloat16)
    dquery = jnp.einsum("hlm,mhe->lhe", dscore, keys, preferred_element_type=jnp.float32) * scale
    dkeys = jnp.einsum("hlm,lhe->mhe", dscore, query, preferred_element_type=jnp.float32) * scale
    dvalues = jnp.einsum(
        "hlm,lhe->mhe", probs.astype(jnp.bfloat16), grad_out, preferred_element_type=jnp.float32
    )
    return (dquery, dkeys, dvalues)


def local(tokens, prefix, qkv_weight, out_weight, in_weight, down_weight, cotangent):
    micro = tokens.shape[0]
    length = tokens.shape[2]
    width = tokens.shape[3]
    hidden_units = down_weight.shape[0] * lax.axis_size("shard")
    scale = HD ** (-0.5)
    cosine, sine = rope_tables(length, HD)
    row_pos = lax.broadcasted_iota(jnp.int32, (length, length), 0)
    col_pos = lax.broadcasted_iota(jnp.int32, (length, length), 1)
    full_set = (
        lax.all_gather(qkv_weight, "shard", axis=0, tiled=True),
        lax.all_gather(out_weight, "shard", axis=0, tiled=True),
        lax.all_gather(in_weight, "shard", axis=0, tiled=True),
        lax.all_gather(down_weight, "shard", axis=0, tiled=True),
    )
    outputs = []
    grad_inputs = []
    kept_h1, kept_gqkv, kept_attn, kept_ga, kept_h2, kept_ggu, kept_hid, kept_gm = (
        [],
        [],
        [],
        [],
        [],
        [],
        [],
        [],
    )
    for batch_index in range(micro):
        xrow = tokens[batch_index, 0].astype(jnp.float32)
        normed_one, inverse_one = norm_rows(xrow)
        first_in = normed_one.astype(jnp.bfloat16)
        mixed = jnp.dot(first_in, full_set[0], preferred_element_type=jnp.float32)
        query = rotate(mixed[:, :width].reshape(length, H, HD), cosine, sine).astype(jnp.bfloat16)
        keys = rotate(mixed[:, width : 2 * width].reshape(length, H, HD), cosine, sine).astype(
            jnp.bfloat16
        )
        values = mixed[:, 2 * width :].reshape(length, H, HD).astype(jnp.bfloat16)
        allowed = (col_pos <= row_pos) | (col_pos < prefix[batch_index, 0])
        attended, log_total = attend(query, keys, values, allowed, scale)
        attn_low = attended.reshape(length, width).astype(jnp.bfloat16)
        middle = xrow + jnp.dot(attn_low, full_set[1], preferred_element_type=jnp.float32)
        normed_two, inverse_two = norm_rows(middle)
        second_in = normed_two.astype(jnp.bfloat16)
        gate_up = jnp.dot(second_in, full_set[2], preferred_element_type=jnp.float32)
        up_part = gate_up[:, :hidden_units]
        gate_part = gate_up[:, hidden_units:]
        sigmoid = jax.nn.sigmoid(gate_part)
        hidden = (gate_part * sigmoid * up_part).astype(jnp.bfloat16)
        final = middle + jnp.dot(hidden, full_set[3], preferred_element_type=jnp.float32)
        outputs.append(final.astype(jnp.bfloat16))
        grad_final = cotangent[batch_index, 0].astype(jnp.float32)
        grad_m = grad_final.astype(jnp.bfloat16)
        grad_hidden = transpose_dot(grad_m, full_set[3])
        grad_up = grad_hidden * (gate_part * sigmoid)
        grad_gate = grad_hidden * up_part * (sigmoid * (1.0 + gate_part * (1.0 - sigmoid)))
        grad_gu = jnp.concatenate([grad_up, grad_gate], axis=-1).astype(jnp.bfloat16)
        grad_mid = grad_final + norm_back(
            normed_two, inverse_two, transpose_dot(grad_gu, full_set[2])
        )
        grad_branch = grad_mid.astype(jnp.bfloat16)
        grad_att = transpose_dot(grad_branch, full_set[1]).astype(jnp.bfloat16)
        dquery, dkeys, dvalues = attend_back(
            query, keys, values, log_total, grad_att.reshape(length, H, HD), allowed, scale
        )
        dquery = rotate_back(dquery, cosine, sine).reshape(length, width)
        dkeys = rotate_back(dkeys, cosine, sine).reshape(length, width)
        grad_mixed = jnp.concatenate(
            [dquery, dkeys, dvalues.reshape(length, width)], axis=-1
        ).astype(jnp.bfloat16)
        grad_input = grad_mid + norm_back(
            normed_one, inverse_one, transpose_dot(grad_mixed, full_set[0])
        )
        grad_inputs.append(grad_input)
        kept_h1.append(first_in)
        kept_gqkv.append(grad_mixed)
        kept_attn.append(attn_low)
        kept_ga.append(grad_branch)
        kept_h2.append(second_in)
        kept_ggu.append(grad_gu)
        kept_hid.append(hidden)
        kept_gm.append(grad_m)
    all_h1 = jnp.concatenate(kept_h1, axis=0)
    all_gqkv = jnp.concatenate(kept_gqkv, axis=0)
    all_attn = jnp.concatenate(kept_attn, axis=0)
    all_ga = jnp.concatenate(kept_ga, axis=0)
    all_h2 = jnp.concatenate(kept_h2, axis=0)
    all_ggu = jnp.concatenate(kept_ggu, axis=0)
    all_hid = jnp.concatenate(kept_hid, axis=0)
    all_gm = jnp.concatenate(kept_gm, axis=0)
    part_one = inner_rows(all_h1, all_gqkv)
    part_two = inner_rows(all_attn, all_ga)
    part_three = inner_rows(all_h2, all_ggu)
    row_share = lax.psum_scatter(
        jnp.concatenate([part_one, part_two, part_three], axis=1),
        "shard",
        scatter_dimension=0,
        tiled=True,
    )
    down_share = lax.psum_scatter(
        inner_rows(all_hid, all_gm), "shard", scatter_dimension=0, tiled=True
    )
    grad_qkv, grad_out, grad_in, grad_down = (
        lax.psum(row_share[:, : 3 * width].astype(jnp.bfloat16), "rep").astype(jnp.float32),
        lax.psum(row_share[:, 3 * width : 4 * width].astype(jnp.bfloat16), "rep").astype(
            jnp.float32
        ),
        lax.psum(row_share[:, 4 * width :].astype(jnp.bfloat16), "rep").astype(jnp.float32),
        lax.psum(down_share.astype(jnp.bfloat16), "rep").astype(jnp.float32),
    )
    result = jnp.stack(outputs, axis=0)[:, None]
    grad_tokens = jnp.stack(grad_inputs, axis=0)[:, None]
    return (result, grad_tokens, grad_qkv, grad_out, grad_in, grad_down)


def solution(mesh):
    placed = (
        P(None, ("rep", "shard"), None, None),
        P(None, ("rep", "shard")),
        P("shard", None),
        P("shard", None),
        P("shard", None),
        P("shard", None),
        P(None, ("rep", "shard"), None, None),
    )
    return jax.shard_map(
        local,
        mesh=mesh,
        in_specs=placed,
        out_specs=(
            P(None, ("rep", "shard"), None, None),
            P(None, ("rep", "shard"), None, None),
            P("shard", None),
            P("shard", None),
            P("shard", None),
            P("shard", None),
        ),
        check_vma=False,
    )
```

profile of v0, /device:TPU:0, one launch (start us, length us, event | category | flops | bytes accessed | tf_op | source)
XLA Modules:
  0.0 870.6 jit_solution(7404513328902034223)
XLA Ops:
  10.0 1.3 fusion.149
  13.4 1.1 convert_reduce_fusion.1
  14.6 1.2 fusion.91
  16.0 1.7 slice_bitcast_fusion.1
  17.9 57.0 %all-gather.5.cloned.1.call-done = bf16[1024,3072]{1,0:T(8,128)(2,1)} async-done(((bf16[64,3072]{1,0:T(8,128)(2,1)}), bf16[1024,3072]{1,0:T(8,128)(2,1)}) %all-gather.5.cloned.1.call-update) | async-done | bytes 6291472 | tf_op jit(solution)/shard_map/all_gather | solution.py:96
  74.9 4.0 fusion.154
  79.6 4.0 fusion.156
  83.6 0.9 convert_element_type.150
  85.2 1.3 fusion.55
  87.9 29.1 %all-gather.7.cloned.1.call-done = bf16[1024,1024]{1,0:T(8,128)(2,1)} async-done(((bf16[64,1024]{1,0:T(8,128)(2,1)}), bf16[1024,1024]{1,0:T(8,128)(2,1)}) %all-gather.7.cloned.1.call-update) | async-done | bytes 2097168 | tf_op jit(solution)/shard_map/all_gather | solution.py:97
  117.0 2.3 fusion.153
  119.6 1.3 fusion.150
  123.6 88.8 %all-gather.9.cloned.1.call-done = bf16[1024,5632]{1,0:T(8,128)(2,1)} async-done(((bf16[64,5632]{1,0:T(8,128)(2,1)}), bf16[1024,5632]{1,0:T(8,128)(2,1)}) %all-gather.9.cloned.1.call-update) | async-done | bytes 11534352 | tf_op jit(solution)/shard_map/all_gather | solution.py:98
  212.4 7.7 fusion.157
  220.2 3.3 fusion.155
  223.5 48.3 %all-gather.11.cloned.1.call-done = bf16[2816,1024]{1,0:T(8,128)(2,1)} async-done(((bf16[176,1024]{1,0:T(8,128)(2,1)}), bf16[2816,1024]{1,0:T(8,128)(2,1)}) %all-gather.11.cloned.1.call-update) | async-done | bytes 5767184 | tf_op jit(solution)/shard_map/all_gather | solution.py:99
  271.8 5.9 multiply_convert_fusion.1
  277.8 2.8 multiply_convert_fusion.3
  280.6 0.8 copy-done.20
  281.3 6.1 fusion.46
  289.0 8.9 %fusion.140 = (f32[64]{0:T(128)S(1)}, f32[64]{0:T(128)S(1)}, f32[64,1024]{1,0:T(8,128)S(1)}) fusion(f32[64]{0:T(128)} %copy-done.65, f32[64,1024]{1,0:T(8,128)} %copy-done.3, f32[64]{0:T(128)} %copy-done.57, bf16[1024,5632]{1,0:T(8,128)(2,1)} %all-gather.9.cloned.1.call-done, bf16[64,2816]{1,0:T(8,128)(2,1)} %get-tuple-element.35, ...), kind=kOutput, calls=%fused_computation.237 | convolution fusion | flops 739966848 | bytes 12780544 | tf_op jit(solution)/shard_map/dot_general | solution.py:47
  298.0 9.5 %fusion.139 = (f32[64]{0:T(128)S(1)}, f32[64]{0:T(128)S(1)}, f32[64,1024]{1,0:T(8,128)S(1)}) fusion(f32[64]{0:T(128)S(1)} %copy-done.64, f32[64,1024]{1,0:T(8,128)S(1)} %get-tuple-element.91, f32[64]{0:T(128)S(1)} %copy-done.56, bf16[1024,5632]{1,0:T(8,128)(2,1)} %all-gather.9.cloned.1.call-done, bf16[64,2816]{1,0:T(8,128)(2,1)S(1)} %copy-done.26, ...), kind=kOutput, calls=%fused_computation.236 | convolution fusion | flops 739966848 | bytes 12780544 | tf_op jit(solution)/shard_map/dot_general | solution.py:47
  307.6 1.1 fusion.141
  309.3 1.4 convolution_convert_fusion.4
  310.7 1.8 copy.66
  312.5 2.3 convolution_convert_fusion.5
  314.8 1.1 copy.65
  316.0 1.9 fusion.97
  321.8 6.5 fusion.26
  328.3 10.9 %fusion = f32[1024,5632]{1,0:T(8,128)} fusion(bf16[64,2816]{1,0:T(8,128)(2,1)S(1)} %copy-done.23, bf16[64,2816]{1,0:T(8,128)(2,1)S(1)} %copy-done.22, bf16[64,2816]{1,0:T(8,128)(2,1)S(1)} %copy-done.27, bf16[64,2816]{1,0:T(8,128)(2,1)S(1)} %copy-done.25, bf16[64,1024]{1,0:T(8,128)(2,1)S(1)} %copy-done.16, bf16[64,1024]{1,0:T(8,128)(2,1)S(1)} %fusion.122), kind=kOutput, calls=%fused_computation.1 | convolution fusion | flops 1482686464 | bytes 24772608 | tf_op jit(solution)/shard_map/dot_general | solution.py:53
  339.2 26.3 %pad_maximum_fusion = f32[1024,9728]{1,0:T(8,128)} fusion(f32[1024,5632]{1,0:T(8,128)} %fusion, f32[1024,1024]{1,0:T(8,128)S(1)} %fusion.97, f32[1024,3072]{1,0:T(8,128)} %fusion.26), kind=kLoop, calls=%fused_computation | loop fusion | flops 19922944 | bytes 79691776 | tf_op jit(solution)/shard_map/concatenate | solution.py:179
  365.6 0.9 copy-done.5
  366.6 3.9 fusion.12
  370.5 3.9 fusion.13
  375.1 4.8 fusion.20
  380.0 32.5 %reduce-scatter.5.cloned.1.call-done = f32[176,1024]{1,0:T(8,128)} async-done(((f32[2816,1024]{1,0:T(8,128)}), f32[176,1024]{1,0:T(8,128)}) %reduce-scatter.5.cloned.1.call-update) | async-done | bytes 720912 | tf_op jit(solution)/shard_map/reduce_scatter | solution.py:184
  412.5 1.9 convert_element_type.173
  414.4 386.4 %reduce-scatter.3.cloned.1.call-done = f32[64,9728]{1,0:T(8,128)} async-done(((f32[1024,9728]{1,0:T(8,128)}), f32[64,9728]{1,0:T(8,128)}) %reduce-scatter.3.cloned.1.call-update) | async-done | bytes 2490384 | tf_op jit(solution)/shard_map/reduce_scatter | solution.py:178
  800.7 1.8 convert.61
  803.3 0.8 slice.171
  804.1 0.9 slice.173
  805.1 5.0 fusion.138
  810.4 0.8 maximum_bitcast_fusion
  811.2 45.8 %all-reduce.3.cloned.1.call-done = (bf16[64,3072]{1,0:T(8,128)(2,1)}, bf16[64,1024]{1,0:T(8,128)(2,1)}, bf16[64,5632]{1,0:T(8,128)(2,1)}, bf16[176,1024]{1,0:T(8,128)(2,1)}) async-done(((bf16[64,3072]{1,0:T(8,128)(2,1)}, bf16[64,1024]{1,0:T(8,128)(2,1)}, bf16[64,5632]{1,0:T(8,128)(2,1)}, bf16[176,1024]{1,0:T(8,128)(2,1)}), (bf16[64,3072]{1,0:T(8,128)(2,1)}, bf16[64,1024]{1,0:T(8,128)(2,1)}, ...) | async-done | bytes 1605648 | tf_op jit(solution)/shard_map/psum | solution.py:188
  857.0 1.7 convert_element_type.171
  858.7 1.9 convert_element_type.170
  860.7 1.9 convert_element_type.174
  862.6 1.2 convert_element_type.172
  (212 shorter events, 18.6 us)
Async XLA Ops:
  7.2 10.5 %copy-start.6 = (bf16[2,1,64,1024]{3,2,1,0:T(8,128)(2,1)S(1)}, bf16[2,1,64,1024]{3,2,1,0:T(8,128)(2,1)}, u32[]{:S(2)}) copy-start(bf16[2,1,64,1024]{3,2,1,0:T(8,128)(2,1)} %param.7) | copy-start | bytes 786436
  7.2 67.7 %all-gather.5.cloned.1.call-start = ((), (), s32[]{:S(2)}) async-start(), calls=%async_computation.2 | async-start | bytes 6684672 | tf_op jit(solution)/shard_map/all_gather | solution.py:96
  7.9 109.1 %all-gather.7.cloned.1.call-start = ((), (), s32[]{:S(2)}) async-start(), calls=%async_computation.3 | async-start | bytes 2228224 | tf_op jit(solution)/shard_map/all_gather | solution.py:97
  8.7 203.8 %all-gather.9.cloned.1.call-start = ((), (), s32[]{:S(2)}) async-start(), calls=%async_computation.4 | async-start | bytes 12255232 | tf_op jit(solution)/shard_map/all_gather | solution.py:98
  9.4 262.4 %all-gather.11.cloned.1.call-start = ((), (), s32[]{:S(2)}) async-start(), calls=%async_computation.5 | async-start | bytes 6127616 | tf_op jit(solution)/shard_map/all_gather | solution.py:99
  10.0 402.5 %reduce-scatter.5.cloned.1.call-start = ((), (), s32[]{:S(2)}) async-start(), calls=%async_computation.7 | async-start | bytes 12255232 | tf_op jit(solution)/shard_map/reduce_scatter | solution.py:184
  14.6 60.3 %copy-start.51 = (f32[64]{0:T(128)}, f32[64]{0:T(128)S(1)}, u32[]{:S(2)}) copy-start(f32[64]{0:T(128)S(1)} %get-tuple-element.100) | copy-start | bytes 772
  14.6 60.3 %copy-start.53 = (f32[64]{0:T(128)}, f32[64]{0:T(128)S(1)}, u32[]{:S(2)}) copy-start(f32[64]{0:T(128)S(1)} %get-tuple-element.101) | copy-start | bytes 772
  15.8 59.1 %copy-start.59 = (f32[64]{0:T(128)}, f32[64]{0:T(128)S(1)}, u32[]{:S(2)}) copy-start(f32[64]{0:T(128)S(1)} %add_rsqrt_fusion.3) | copy-start | bytes 772
  15.8 59.1 %copy-start.61 = (f32[64]{0:T(128)}, f32[64]{0:T(128)S(1)}, u32[]{:S(2)}) copy-start(f32[64]{0:T(128)S(1)} %add_rsqrt_fusion.1) | copy-start | bytes 772
  17.9 61.0 %copy-start.28 = (bf16[64,1024]{1,0:T(8,128)(2,1)}, bf16[64,1024]{1,0:T(8,128)(2,1)S(1)}, u32[]{:S(2)}) copy-start(bf16[64,1024]{1,0:T(8,128)(2,1)S(1)} %get-tuple-element.64) | copy-start | bytes 393220
  17.9 61.7 %copy-start.30 = (bf16[64,1024]{1,0:T(8,128)(2,1)}, bf16[64,1024]{1,0:T(8,128)(2,1)S(1)}, u32[]{:S(2)}) copy-start(bf16[64,1024]{1,0:T(8,128)(2,1)S(1)} %get-tuple-element.65) | copy-start | bytes 393220
  79.1 8.5 copy-start.35
  87.6 32.0 %copy-start.49 = (f32[16,64]{1,0:T(8,128)}, f32[16,64]{1,0:T(8,128)S(1)}, u32[]{:S(2)}) copy-start(f32[16,64]{1,0:T(8,128)S(1)} %fusion.64) | copy-start | bytes 12292
  87.9 31.7 %copy-start.33 = (bf16[16,64,64]{2,1,0:T(8,128)(2,1)}, bf16[16,64,64]{2,1,0:T(8,128)(2,1)S(1)}, u32[]{:S(2)}) copy-start(bf16[16,64,64]{2,1,0:T(8,128)(2,1)S(1)} %convolution_convert_fusion.3) | copy-start | bytes 393220
  117.0 4.0 copy-start.37
  117.0 4.4 copy-start.1
  117.0 4.4 copy-start.7
  119.4 2.9 copy-start.55
  212.4 7.8 copy-start
  271.8 5.9 copy-start.2
  271.8 5.9 copy-start.17
  271.8 5.9 copy-start.41
  277.8 2.8 copy-start.18
  277.8 3.6 copy-start.44
  277.8 3.6 copy-start.45
  287.5 513.3 %reduce-scatter.3.cloned.1.call-start = ((), (), s32[]{:S(2)}) async-start(), calls=%async_computation.6 | async-start | bytes 42336256 | tf_op jit(solution)/shard_map/reduce_scatter | solution.py:178
  289.0 9.0 %copy-start.24 = (bf16[64,2816]{1,0:T(8,128)(2,1)S(1)}, bf16[64,2816]{1,0:T(8,128)(2,1)}, u32[]{:S(2)}) copy-start(bf16[64,2816]{1,0:T(8,128)(2,1)} %get-tuple-element.32) | copy-start | bytes 1081348
  289.0 9.0 %copy-start.26 = (bf16[64,2816]{1,0:T(8,128)(2,1)S(1)}, bf16[64,2816]{1,0:T(8,128)(2,1)}, u32[]{:S(2)}) copy-start(bf16[64,2816]{1,0:T(8,128)(2,1)} %get-tuple-element.33) | copy-start | bytes 1081348
  289.0 9.0 %copy-start.56 = (f32[64]{0:T(128)S(1)}, f32[64]{0:T(128)}, u32[]{:S(2)}) copy-start(f32[64]{0:T(128)} %copy-done.55) | copy-start | bytes 772
  289.0 9.0 %copy-start.64 = (f32[64]{0:T(128)S(1)}, f32[64]{0:T(128)}, u32[]{:S(2)}) copy-start(f32[64]{0:T(128)} %copy-done.63) | copy-start | bytes 772
  298.0 9.6 %copy-start.4 = (f32[64,1024]{1,0:T(8,128)S(1)}, f32[64,1024]{1,0:T(8,128)}, u32[]{:S(2)}) copy-start(f32[64,1024]{1,0:T(8,128)} %copy-done.3) | copy-start | bytes 786436
  298.0 9.6 %copy-start.42 = (bf16[2,1,64,1024]{3,2,1,0:T(8,128)(2,1)S(1)}, bf16[2,1,64,1024]{3,2,1,0:T(8,128)(2,1)}, u32[]{:S(2)}) copy-start(bf16[2,1,64,1024]{3,2,1,0:T(8,128)(2,1)} %param.13) | copy-start | bytes 786436
  298.0 9.6 %copy-start.58 = (f32[64]{0:T(128)S(1)}, f32[64]{0:T(128)}, u32[]{:S(2)}) copy-start(f32[64]{0:T(128)} %copy-done.57) | copy-start | bytes 772
  298.0 9.6 %copy-start.66 = (f32[64]{0:T(128)S(1)}, f32[64]{0:T(128)}, u32[]{:S(2)}) copy-start(f32[64]{0:T(128)} %copy-done.65) | copy-start | bytes 772
  314.8 3.1 copy-start.9
  314.8 3.1 copy-start.38
  321.8 6.5 copy-start.16
  321.8 6.5 copy-start.22
  321.8 6.5 copy-start.23
  321.8 6.5 copy-start.25
  321.8 6.5 copy-start.27
  365.5 5.0 copy-start.21
  365.6 491.5 %all-reduce.3.cloned.1.call-start = ((), (), s32[]{:S(2)}) async-start(), calls=%async_computation.8 | async-start | bytes 3211264 | tf_op jit(solution)/shard_map/psum | solution.py:188
  802.6 2.4 copy-start.8
  805.0 5.1 copy-start.39
  805.0 5.1 copy-start.40
  857.0 5.5 copy-start.43
  (26 other events, 31.8 us)
Sparse Core Ops, SparseCore 0:
  10.3 64.5 all-gather.4
  77.0 39.9 all-gather.6
  119.3 93.0 all-gather.8
  214.6 57.1 all-gather.10
  287.6 124.8 reduce-scatter.4
  417.3 383.4 reduce-scatter.2
  805.1 51.8 all-reduce.2
where the time goes:
time: 871 us
  waiting for transfers between devices  690 us (79%)
  matrix products  100 us (11%)
  other arithmetic  49.7 us (6%)
  between operations  15.2 us (2%)
  local copies, waits for them, and re-layouts  14.9 us (2%)
    reduce_scatter x1, waiting for transfers between devices, local(): lax.psum_scatter(jnp.concatenate([part_one, part_two, part_three], axis=1...  386 us
    all_gather x1, waiting for transfers between devices, local(): lax.all_gather(in_weight, 'shard', axis=0, tiled=True)  88.8 us
    all_gather x1, waiting for transfers between devices, local(): lax.all_gather(qkv_weight, 'shard', axis=0, tiled=True)  57 us
    all_gather x1, waiting for transfers between devices, local(): lax.all_gather(down_weight, 'shard', axis=0, tiled=True)  48.3 us
    psum x1, waiting for transfers between devices, local(): lax.psum(row_share[:, :3 * width].astype(jnp.bfloat16), 'rep')  45.8 us
    dot_general x8, matrix products, transpose_dot(): lax.dot_general(left, right, (((1,), (1,)), ((), ())), preferred_element_...  40.7 us
    reduce_scatter x1, waiting for transfers between devices, local(): lax.psum_scatter(inner_rows(all_hid, all_gm), 'shard', scatter_dimension=...  32.5 us
    all_gather x1, waiting for transfers between devices, local(): lax.all_gather(out_weight, 'shard', axis=0, tiled=True)  29.1 us
  transfers between devices with their start and end apart: 7, of which 7 were waited for; matrix products, arithmetic and copies ran while one was open for 15% of the time, Pallas kernels for 0%

commit v1 on v0

--- a/solution.py
+++ b/solution.py
@@ -5,6 +5,17 @@
 
 H = 16
 HD = 64
+
+
+def collect(value, axis, dim):
+    ways = lax.axis_size(axis)
+    pieces = [value]
+    for far in range(1, ways):
+        pieces.append(
+            lax.ppermute(pieces[far - 1], axis, [(d, (d - 1) % ways) for d in range(ways)])
+        )
+    line = jnp.concatenate(pieces, axis=dim)
+    return jnp.roll(line, lax.axis_index(axis) * value.shape[dim], axis=dim)
 
 
 def norm_rows(values):
@@ -93,7 +104,7 @@
     row_pos = lax.broadcasted_iota(jnp.int32, (length, length), 0)
     col_pos = lax.broadcasted_iota(jnp.int32, (length, length), 1)
     full_set = (
-        lax.all_gather(qkv_weight, "shard", axis=0, tiled=True),
+        collect(qkv_weight, "shard", 0),
         lax.all_gather(out_weight, "shard", axis=0, tiled=True),
         lax.all_gather(in_weight, "shard", axis=0, tiled=True),
         lax.all_gather(down_weight, "shard", axis=0, tiled=True),

time: 871 us -> 869 us (level)
  waiting for transfers between devices: 690 us -> 608 us
  starting transfers between devices: 0.27 us -> 70.4 us
    ppermute x0 -> x15, waiting for transfers between devices: none -> 138 us  [collect(): lax.ppermute(pieces[far - 1], axis, [(d, (d - 1) % ways) for d in range(w...]
    all_gather x1, waiting for transfers between devices: 88.8 us -> 0.02 us  [local(): lax.all_gather(in_weight, 'shard', axis=0, tiled=True)]
    ppermute x0 -> x15, starting transfers between devices: none -> 70.2 us  [collect(): lax.ppermute(pieces[far - 1], axis, [(d, (d - 1) % ways) for d in range(w...]
    all_gather x1 -> x0, waiting for transfers between devices: 57 us -> none  [local(): lax.all_gather(qkv_weight, 'shard', axis=0, tiled=True)]
    all_gather x1, waiting for transfers between devices: 48.3 us -> 0.02 us  [local(): lax.all_gather(down_weight, 'shard', axis=0, tiled=True)]
    all_gather x1, waiting for transfers between devices: 29.1 us -> 0.02 us  [local(): lax.all_gather(out_weight, 'shard', axis=0, tiled=True)]
  transfers between devices with their start and end apart: 7 -> 21, of which waited for: 7 -> 18; matrix products, arithmetic and copies ran while one was open for 15% -> 16% of each run, Pallas kernels for 0% -> 0%
where the time goes in v1:
time: 869 us; the launch traced here: 868 us
  waiting for transfers between devices  608 us (70%)
  matrix products  105 us (12%)
  starting transfers between devices  70.4 us (8%)
  other arithmetic  49.5 us (6%)
  local copies, waits for them, and re-layouts  19.5 us (2%)
  between operations  15.4 us (2%)
    reduce_scatter x1, waiting for transfers between devices, local(): lax.psum_scatter(jnp.concatenate([part_one, part_two, part_three], axis=1...  386 us
    ppermute x15, waiting for transfers between devices, collect(): lax.ppermute(pieces[far - 1], axis, [(d, (d - 1) % ways) for d in range(w...  138 us
    ppermute x15, starting transfers between devices, collect(): lax.ppermute(pieces[far - 1], axis, [(d, (d - 1) % ways) for d in range(w...  70.2 us
    psum x1, waiting for transfers between devices, local(): lax.psum(row_share[:, :3 * width].astype(jnp.bfloat16), 'rep')  45.2 us
    dot_general x8, matrix products, transpose_dot(): lax.dot_general(left, right, (((1,), (1,)), ((), ())), preferred_element_...  43.4 us
    reduce_scatter x1, waiting for transfers between devices, local(): lax.psum_scatter(inner_rows(all_hid, all_gm), 'shard', scatter_dimension=...  36.9 us
    dot_general x4, matrix products, inner_rows(): lax.dot_general(left, right, (((0,), (0,)), ((), ())), preferred_element_...  25.4 us
    concatenate x1, other arithmetic, local(): jnp.concatenate([part_one, part_two, part_three], axis=1)  24.9 us
  transfers between devices with their start and end apart: 21, of which 18 were waited for; matrix products, arithmetic and copies ran while one was open for 16% of the time, Pallas kernels for 0%

profile of v1, /device:TPU:0, one launch (start us, length us, event | category | flops | bytes accessed | tf_op | source)
XLA Modules:
  0.0 868.2 jit_solution(12692442344748588357)
XLA Ops:
  8.7 5.5 collective-permute-start
  14.2 5.6 collective-permute-done
  19.8 4.5 collective-permute-start.1
  26.4 5.9 collective-permute-done.1
  32.2 4.6 collective-permute-start.2
  38.7 8.4 collective-permute-done.2
  47.1 4.7 collective-permute-start.3
  52.4 4.8 collective-permute-done.3
  57.2 4.6 collective-permute-start.4
  63.1 4.0 collective-permute-done.4
  67.1 4.6 collective-permute-start.5
  73.4 12.0 %collective-permute-done.5 = bf16[64,3072]{1,0:T(8,128)(2,1)S(1)} collective-permute-done((bf16[64,3072]{1,0:T(8,128)(2,1)S(1)}, bf16[64,3072]{1,0:T(8,128)(2,1)S(1)}, u32[]{:S(2)}, u32[]{:S(2)}) %collective-permute-start.5) | collective-permute-done | bytes 393248 | tf_op jit(solution)/shard_map/ppermute | solution.py:15
  85.4 4.7 collective-permute-start.6
  92.0 7.7 collective-permute-done.6
  99.7 4.7 collective-permute-start.7
  106.3 11.3 %collective-permute-done.7 = bf16[64,3072]{1,0:T(8,128)(2,1)S(1)} collective-permute-done((bf16[64,3072]{1,0:T(8,128)(2,1)S(1)}, bf16[64,3072]{1,0:T(8,128)(2,1)S(1)}, u32[]{:S(2)}, u32[]{:S(2)}) %collective-permute-start.7) | collective-permute-done | bytes 393248 | tf_op jit(solution)/shard_map/ppermute | solution.py:15
  117.6 4.6 collective-permute-start.8
  122.3 13.6 %collective-permute-done.8 = bf16[64,3072]{1,0:T(8,128)(2,1)S(1)} collective-permute-done((bf16[64,3072]{1,0:T(8,128)(2,1)S(1)}, bf16[64,3072]{1,0:T(8,128)(2,1)S(1)}, u32[]{:S(2)}, u32[]{:S(2)}) %collective-permute-start.8) | collective-permute-done | bytes 393248 | tf_op jit(solution)/shard_map/ppermute | solution.py:15
  135.9 4.7 collective-permute-start.9
  140.6 12.1 %collective-permute-done.9 = bf16[64,3072]{1,0:T(8,128)(2,1)S(1)} collective-permute-done((bf16[64,3072]{1,0:T(8,128)(2,1)S(1)}, bf16[64,3072]{1,0:T(8,128)(2,1)S(1)}, u32[]{:S(2)}, u32[]{:S(2)}) %collective-permute-start.9) | collective-permute-done | bytes 393248 | tf_op jit(solution)/shard_map/ppermute | solution.py:15
  152.7 4.7 collective-permute-start.10
  157.4 11.4 %collective-permute-done.10 = bf16[64,3072]{1,0:T(8,128)(2,1)S(1)} collective-permute-done((bf16[64,3072]{1,0:T(8,128)(2,1)S(1)}, bf16[64,3072]{1,0:T(8,128)(2,1)S(1)}, u32[]{:S(2)}, u32[]{:S(2)}) %collective-permute-start.10) | collective-permute-done | bytes 393248 | tf_op jit(solution)/shard_map/ppermute | solution.py:15
  168.9 4.6 collective-permute-start.11
  173.5 5.2 collective-permute-done.11
  178.8 4.6 collective-permute-start.12
  183.4 13.6 %collective-permute-done.12 = bf16[64,3072]{1,0:T(8,128)(2,1)S(1)} collective-permute-done((bf16[64,3072]{1,0:T(8,128)(2,1)S(1)}, bf16[64,3072]{1,0:T(8,128)(2,1)S(1)}, u32[]{:S(2)}, u32[]{:S(2)}) %collective-permute-start.12) | collective-permute-done | bytes 393248 | tf_op jit(solution)/shard_map/ppermute | solution.py:15
  197.0 4.6 collective-permute-start.13
  201.7 9.1 %collective-permute-done.13 = bf16[64,3072]{1,0:T(8,128)(2,1)S(1)} collective-permute-done((bf16[64,3072]{1,0:T(8,128)(2,1)S(1)}, bf16[64,3072]{1,0:T(8,128)(2,1)S(1)}, u32[]{:S(2)}, u32[]{:S(2)}) %collective-permute-start.13) | collective-permute-done | bytes 393248 | tf_op jit(solution)/shard_map/ppermute | solution.py:15
  210.8 4.7 collective-permute-start.14
  215.5 13.7 %collective-permute-done.14 = bf16[64,3072]{1,0:T(8,128)(2,1)S(1)} collective-permute-done((bf16[64,3072]{1,0:T(8,128)(2,1)S(1)}, bf16[64,3072]{1,0:T(8,128)(2,1)S(1)}, u32[]{:S(2)}, u32[]{:S(2)}) %collective-permute-start.14) | collective-permute-done | bytes 393248 | tf_op jit(solution)/shard_map/ppermute | solution.py:15
  229.8 4.6 copy-done.1
  237.0 4.1 fusion.6
  253.1 7.6 fusion.165
  262.9 5.8 multiply_convert_fusion.1
  268.7 5.6 multiply_convert_fusion.3
  275.0 6.1 fusion.52
  281.4 8.3 fusion.150
  289.7 9.9 %fusion.149 = (f32[64]{0:T(128)S(1)}, f32[64]{0:T(128)S(1)}, f32[64,1024]{1,0:T(8,128)S(1)}) fusion(f32[64]{0:T(128)} %copy-done.53, f32[64,1024]{1,0:T(8,128)S(1)} %get-tuple-element.91, f32[64]{0:T(128)} %copy-done.45, bf16[1024,5632]{1,0:T(8,128)(2,1)} %all-gather.6.cloned.1.call-done, bf16[64,2816]{1,0:T(8,128)(2,1)} %get-tuple-element.33, ...), kind=kOutput, calls=%fused_computation.278 | convolution fusion | flops 739966848 | bytes 12780544 | tf_op jit(solution)/shard_map/dot_general | solution.py:58
  317.1 6.4 fusion.32
  323.5 11.0 %fusion.8 = f32[1024,5632]{1,0:T(8,128)} fusion(bf16[64,2816]{1,0:T(8,128)(2,1)S(1)} %copy-done.21, bf16[64,2816]{1,0:T(8,128)(2,1)S(1)} %copy-done.20, bf16[64,2816]{1,0:T(8,128)(2,1)S(1)} %copy-done.23, bf16[64,2816]{1,0:T(8,128)(2,1)S(1)} %copy-done.22, bf16[64,1024]{1,0:T(8,128)(2,1)S(1)} %copy-done.14, bf16[64,1024]{1,0:T(8,128)(2,1)S(1)} %fusion.128), kind=kOutput, calls=%fused_computation.9 | convolution fusion | flops 1482686464 | bytes 24772608 | tf_op jit(solution)/shard_map/dot_general | solution.py:64
  334.5 24.9 %pad_maximum_fusion = f32[1024,9728]{1,0:T(8,128)} fusion(f32[1024,5632]{1,0:T(8,128)} %fusion.8, f32[1024,1024]{1,0:T(8,128)S(1)} %fusion.103, f32[1024,3072]{1,0:T(8,128)} %fusion.32), kind=kLoop, calls=%fused_computation | loop fusion | flops 19922944 | bytes 79691776 | tf_op jit(solution)/shard_map/concatenate | solution.py:190
  359.5 5.0 fusion
  364.6 3.8 fusion.20
  368.5 3.8 fusion.21
  372.3 36.9 %reduce-scatter.5.cloned.1.call-done = f32[176,1024]{1,0:T(8,128)} async-done(((f32[2816,1024]{1,0:T(8,128)}), f32[176,1024]{1,0:T(8,128)}) %reduce-scatter.5.cloned.1.call-update) | async-done | bytes 720912 | tf_op jit(solution)/shard_map/reduce_scatter | solution.py:195
  411.1 386.3 %reduce-scatter.3.cloned.1.call-done = f32[64,9728]{1,0:T(8,128)} async-done(((f32[1024,9728]{1,0:T(8,128)}), f32[64,9728]{1,0:T(8,128)}) %reduce-scatter.3.cloned.1.call-update) | async-done | bytes 2490384 | tf_op jit(solution)/shard_map/reduce_scatter | solution.py:189
  802.3 5.0 fusion.148
  808.4 45.2 %all-reduce.3.cloned.1.call-done = (bf16[64,3072]{1,0:T(8,128)(2,1)}, bf16[64,1024]{1,0:T(8,128)(2,1)}, bf16[64,5632]{1,0:T(8,128)(2,1)}, bf16[176,1024]{1,0:T(8,128)(2,1)}) async-done(((bf16[64,3072]{1,0:T(8,128)(2,1)}, bf16[64,1024]{1,0:T(8,128)(2,1)}, bf16[64,5632]{1,0:T(8,128)(2,1)}, bf16[176,1024]{1,0:T(8,128)(2,1)}), (bf16[64,3072]{1,0:T(8,128)(2,1)}, bf16[64,1024]{1,0:T(8,128)(2,1)}, ...) | async-done | bytes 1605648 | tf_op jit(solution)/shard_map/psum | solution.py:199
  (251 shorter events, 63.9 us)
Async XLA Ops:
  7.2 222.0 %copy-start.15 = (bf16[64,3072]{1,0:T(8,128)(2,1)S(1)}, bf16[64,3072]{1,0:T(8,128)(2,1)}, u32[]{:S(2)}) copy-start(bf16[64,3072]{1,0:T(8,128)(2,1)} %param.9) | copy-start | bytes 1179652
  7.2 237.5 %all-gather.4.cloned.1.call-start = ((), (), s32[]{:S(2)}) async-start(), calls=%async_computation.2 | async-start | bytes 2228224 | tf_op jit(solution)/shard_map/all_gather | solution.py:108
  7.9 245.1 %all-gather.6.cloned.1.call-start = ((), (), s32[]{:S(2)}) async-start(), calls=%async_computation.3 | async-start | bytes 12255232 | tf_op jit(solution)/shard_map/all_gather | solution.py:109
  8.7 254.2 %all-gather.8.cloned.1.call-start = ((), (), s32[]{:S(2)}) async-start(), calls=%async_computation.4 | async-start | bytes 6127616 | tf_op jit(solution)/shard_map/all_gather | solution.py:110
  8.7 11.1 %collective-permute-start = (bf16[64,3072]{1,0:T(8,128)(2,1)}, bf16[64,3072]{1,0:T(8,128)(2,1)S(1)}, u32[]{:S(2)}, u32[]{:S(2)}) collective-permute-start(bf16[64,3072]{1,0:T(8,128)(2,1)} %param.9), channel_id=1, source_target_pairs={{0,15},{1,0},{2,1},{3,2},{4,3},{5,4},{6,5},{7,6},{8,7},{9,8},{10,9... | collective-permute-start | bytes 1179656 | tf_op jit(solution)/shard_map/ppermute | solution.py:15
  19.8 12.4 %collective-permute-start.1 = (bf16[64,3072]{1,0:T(8,128)(2,1)S(1)}, bf16[64,3072]{1,0:T(8,128)(2,1)S(1)}, u32[]{:S(2)}, u32[]{:S(2)}) collective-permute-start(bf16[64,3072]{1,0:T(8,128)(2,1)S(1)} %collective-permute-done), channel_id=1, source_target_pairs={{0,15},{1,0},{2,1},{3,2},{4,3},{5,4},{6,5},{7,6},{8,7},{9,8},{10,9... | collective-permute-start | bytes 1179656 | tf_op jit(solution)/shard_map/ppermute | solution.py:15
  24.3 384.9 %reduce-scatter.5.cloned.1.call-start = ((), (), s32[]{:S(2)}) async-start(), calls=%async_computation.6 | async-start | bytes 12255232 | tf_op jit(solution)/shard_map/reduce_scatter | solution.py:195
  32.2 14.8 %collective-permute-start.2 = (bf16[64,3072]{1,0:T(8,128)(2,1)S(1)}, bf16[64,3072]{1,0:T(8,128)(2,1)S(1)}, u32[]{:S(2)}, u32[]{:S(2)}) collective-permute-start(bf16[64,3072]{1,0:T(8,128)(2,1)S(1)} %collective-permute-done.1), channel_id=1, source_target_pairs={{0,15},{1,0},{2,1},{3,2},{4,3},{5,4},{6,5},{7,6},{8,7},{9,8},{10,9... | collective-permute-start | bytes 1179656 | tf_op jit(solution)/shard_map/ppermute | solution.py:15
  47.1 10.1 %collective-permute-start.3 = (bf16[64,3072]{1,0:T(8,128)(2,1)S(1)}, bf16[64,3072]{1,0:T(8,128)(2,1)S(1)}, u32[]{:S(2)}, u32[]{:S(2)}) collective-permute-start(bf16[64,3072]{1,0:T(8,128)(2,1)S(1)} %collective-permute-done.2), channel_id=1, source_target_pairs={{0,15},{1,0},{2,1},{3,2},{4,3},{5,4},{6,5},{7,6},{8,7},{9,8},{10,9... | collective-permute-start | bytes 1179656 | tf_op jit(solution)/shard_map/ppermute | solution.py:15
  51.7 40.2 %copy-start.41 = (f32[64]{0:T(128)}, f32[64]{0:T(128)S(1)}, u32[]{:S(2)}) copy-start(f32[64]{0:T(128)S(1)} %get-tuple-element.100) | copy-start | bytes 772
  51.7 40.2 %copy-start.43 = (f32[64]{0:T(128)}, f32[64]{0:T(128)S(1)}, u32[]{:S(2)}) copy-start(f32[64]{0:T(128)S(1)} %get-tuple-element.101) | copy-start | bytes 772
  57.2 9.9 %collective-permute-start.4 = (bf16[64,3072]{1,0:T(8,128)(2,1)S(1)}, bf16[64,3072]{1,0:T(8,128)(2,1)S(1)}, u32[]{:S(2)}, u32[]{:S(2)}) collective-permute-start(bf16[64,3072]{1,0:T(8,128)(2,1)S(1)} %collective-permute-done.3), channel_id=1, source_target_pairs={{0,15},{1,0},{2,1},{3,2},{4,3},{5,4},{6,5},{7,6},{8,7},{9,8},{10,9... | collective-permute-start | bytes 1179656 | tf_op jit(solution)/shard_map/ppermute | solution.py:15
  67.1 18.3 %collective-permute-start.5 = (bf16[64,3072]{1,0:T(8,128)(2,1)S(1)}, bf16[64,3072]{1,0:T(8,128)(2,1)S(1)}, u32[]{:S(2)}, u32[]{:S(2)}) collective-permute-start(bf16[64,3072]{1,0:T(8,128)(2,1)S(1)} %collective-permute-done.4), channel_id=1, source_target_pairs={{0,15},{1,0},{2,1},{3,2},{4,3},{5,4},{6,5},{7,6},{8,7},{9,8},{10,9... | collective-permute-start | bytes 1179656 | tf_op jit(solution)/shard_map/ppermute | solution.py:15
  71.7 20.2 %copy-start.49 = (f32[64]{0:T(128)}, f32[64]{0:T(128)S(1)}, u32[]{:S(2)}) copy-start(f32[64]{0:T(128)S(1)} %add_rsqrt_fusion.3) | copy-start | bytes 772
  85.4 14.3 %collective-permute-start.6 = (bf16[64,3072]{1,0:T(8,128)(2,1)S(1)}, bf16[64,3072]{1,0:T(8,128)(2,1)S(1)}, u32[]{:S(2)}, u32[]{:S(2)}) collective-permute-start(bf16[64,3072]{1,0:T(8,128)(2,1)S(1)} %collective-permute-done.5), channel_id=1, source_target_pairs={{0,15},{1,0},{2,1},{3,2},{4,3},{5,4},{6,5},{7,6},{8,7},{9,8},{10,9... | collective-permute-start | bytes 1179656 | tf_op jit(solution)/shard_map/ppermute | solution.py:15
  99.7 17.9 %collective-permute-start.7 = (bf16[64,3072]{1,0:T(8,128)(2,1)S(1)}, bf16[64,3072]{1,0:T(8,128)(2,1)S(1)}, u32[]{:S(2)}, u32[]{:S(2)}) collective-permute-start(bf16[64,3072]{1,0:T(8,128)(2,1)S(1)} %collective-permute-done.6), channel_id=1, source_target_pairs={{0,15},{1,0},{2,1},{3,2},{4,3},{5,4},{6,5},{7,6},{8,7},{9,8},{10,9... | collective-permute-start | bytes 1179656 | tf_op jit(solution)/shard_map/ppermute | solution.py:15
  105.1 129.3 %copy-start.25 = (bf16[64,1024]{1,0:T(8,128)(2,1)S(1)}, bf16[64,1024]{1,0:T(8,128)(2,1)}, u32[]{:S(2)}) copy-start(bf16[64,1024]{1,0:T(8,128)(2,1)} %get-tuple-element.65) | copy-start | bytes 393220
  117.6 18.3 %collective-permute-start.8 = (bf16[64,3072]{1,0:T(8,128)(2,1)S(1)}, bf16[64,3072]{1,0:T(8,128)(2,1)S(1)}, u32[]{:S(2)}, u32[]{:S(2)}) collective-permute-start(bf16[64,3072]{1,0:T(8,128)(2,1)S(1)} %collective-permute-done.7), channel_id=1, source_target_pairs={{0,15},{1,0},{2,1},{3,2},{4,3},{5,4},{6,5},{7,6},{8,7},{9,8},{10,9... | collective-permute-start | bytes 1179656 | tf_op jit(solution)/shard_map/ppermute | solution.py:15
  135.9 16.8 %collective-permute-start.9 = (bf16[64,3072]{1,0:T(8,128)(2,1)S(1)}, bf16[64,3072]{1,0:T(8,128)(2,1)S(1)}, u32[]{:S(2)}, u32[]{:S(2)}) collective-permute-start(bf16[64,3072]{1,0:T(8,128)(2,1)S(1)} %collective-permute-done.8), channel_id=1, source_target_pairs={{0,15},{1,0},{2,1},{3,2},{4,3},{5,4},{6,5},{7,6},{8,7},{9,8},{10,9... | collective-permute-start | bytes 1179656 | tf_op jit(solution)/shard_map/ppermute | solution.py:15
  152.7 16.2 %collective-permute-start.10 = (bf16[64,3072]{1,0:T(8,128)(2,1)S(1)}, bf16[64,3072]{1,0:T(8,128)(2,1)S(1)}, u32[]{:S(2)}, u32[]{:S(2)}) collective-permute-start(bf16[64,3072]{1,0:T(8,128)(2,1)S(1)} %collective-permute-done.9), channel_id=1, source_target_pairs={{0,15},{1,0},{2,1},{3,2},{4,3},{5,4},{6,5},{7,6},{8,7},{9,8},{10,9... | collective-permute-start | bytes 1179656 | tf_op jit(solution)/shard_map/ppermute | solution.py:15
  168.9 9.9 %collective-permute-start.11 = (bf16[64,3072]{1,0:T(8,128)(2,1)S(1)}, bf16[64,3072]{1,0:T(8,128)(2,1)S(1)}, u32[]{:S(2)}, u32[]{:S(2)}) collective-permute-start(bf16[64,3072]{1,0:T(8,128)(2,1)S(1)} %collective-permute-done.10), channel_id=1, source_target_pairs={{0,15},{1,0},{2,1},{3,2},{4,3},{5,4},{6,5},{7,6},{8,7},{9,8},{10,9... | collective-permute-start | bytes 1179656 | tf_op jit(solution)/shard_map/ppermute | solution.py:15
  178.8 18.2 %collective-permute-start.12 = (bf16[64,3072]{1,0:T(8,128)(2,1)S(1)}, bf16[64,3072]{1,0:T(8,128)(2,1)S(1)}, u32[]{:S(2)}, u32[]{:S(2)}) collective-permute-start(bf16[64,3072]{1,0:T(8,128)(2,1)S(1)} %collective-permute-done.11), channel_id=1, source_target_pairs={{0,15},{1,0},{2,1},{3,2},{4,3},{5,4},{6,5},{7,6},{8,7},{9,8},{10,9... | collective-permute-start | bytes 1179656 | tf_op jit(solution)/shard_map/ppermute | solution.py:15
  197.0 13.8 %collective-permute-start.13 = (bf16[64,3072]{1,0:T(8,128)(2,1)S(1)}, bf16[64,3072]{1,0:T(8,128)(2,1)S(1)}, u32[]{:S(2)}, u32[]{:S(2)}) collective-permute-start(bf16[64,3072]{1,0:T(8,128)(2,1)S(1)} %collective-permute-done.12), channel_id=1, source_target_pairs={{0,15},{1,0},{2,1},{3,2},{4,3},{5,4},{6,5},{7,6},{8,7},{9,8},{10,9... | collective-permute-start | bytes 1179656 | tf_op jit(solution)/shard_map/ppermute | solution.py:15
  210.8 18.4 %collective-permute-start.14 = (bf16[64,3072]{1,0:T(8,128)(2,1)S(1)}, bf16[64,3072]{1,0:T(8,128)(2,1)S(1)}, u32[]{:S(2)}, u32[]{:S(2)}) collective-permute-start(bf16[64,3072]{1,0:T(8,128)(2,1)S(1)} %collective-permute-done.13), channel_id=1, source_target_pairs={{0,15},{1,0},{2,1},{3,2},{4,3},{5,4},{6,5},{7,6},{8,7},{9,8},{10,9... | collective-permute-start | bytes 1179656 | tf_op jit(solution)/shard_map/ppermute | solution.py:15
  247.0 13.7 %copy-start.45 = (f32[64]{0:T(128)}, f32[64]{0:T(128)S(1)}, u32[]{:S(2)}) copy-start(f32[64]{0:T(128)S(1)} %broadcast_multiply_fusion.16) | copy-start | bytes 772
  252.2 10.6 %copy-start.47 = (f32[64]{0:T(128)}, f32[64]{0:T(128)S(1)}, u32[]{:S(2)}) copy-start(f32[64]{0:T(128)S(1)} %broadcast_multiply_fusion.14) | copy-start | bytes 772
  253.0 9.8 %copy-start.13 = (bf16[64,1024]{1,0:T(8,128)(2,1)}, bf16[64,1024]{1,0:T(8,128)(2,1)S(1)}, u32[]{:S(2)}) copy-start(bf16[64,1024]{1,0:T(8,128)(2,1)S(1)} %fusion.129) | copy-start | bytes 393220
  262.8 12.2 %copy-start.34 = (bf16[64,1024]{1,0:T(8,128)(2,1)S(1)}, bf16[64,1024]{1,0:T(8,128)(2,1)}, u32[]{:S(2)}) copy-start(bf16[64,1024]{1,0:T(8,128)(2,1)} %get-tuple-element.58) | copy-start | bytes 393220
  262.9 12.2 %copy-start.35 = (bf16[64,1024]{1,0:T(8,128)(2,1)S(1)}, bf16[64,1024]{1,0:T(8,128)(2,1)}, u32[]{:S(2)}) copy-start(bf16[64,1024]{1,0:T(8,128)(2,1)} %get-tuple-element.59) | copy-start | bytes 393220
  268.7 12.5 %copy-start.16 = (bf16[64,2816]{1,0:T(8,128)(2,1)}, bf16[64,2816]{1,0:T(8,128)(2,1)S(1)}, u32[]{:S(2)}) copy-start(bf16[64,2816]{1,0:T(8,128)(2,1)S(1)} %get-tuple-element.37) | copy-start | bytes 1081348
  281.2 516.2 %reduce-scatter.3.cloned.1.call-start = ((), (), s32[]{:S(2)}) async-start(), calls=%async_computation.5 | async-start | bytes 42336256 | tf_op jit(solution)/shard_map/reduce_scatter | solution.py:189
  281.3 18.4 %copy-start.4 = (f32[64,1024]{1,0:T(8,128)S(1)}, f32[64,1024]{1,0:T(8,128)}, u32[]{:S(2)}) copy-start(f32[64,1024]{1,0:T(8,128)} %copy-done.3) | copy-start | bytes 786436
  281.3 18.4 %copy-start.33 = (bf16[2,1,64,1024]{3,2,1,0:T(8,128)(2,1)S(1)}, bf16[2,1,64,1024]{3,2,1,0:T(8,128)(2,1)}, u32[]{:S(2)}) copy-start(bf16[2,1,64,1024]{3,2,1,0:T(8,128)(2,1)} %param.13) | copy-start | bytes 786436
  281.3 18.4 %copy-start.46 = (f32[64]{0:T(128)S(1)}, f32[64]{0:T(128)}, u32[]{:S(2)}) copy-start(f32[64]{0:T(128)} %copy-done.45) | copy-start | bytes 772
  281.3 18.4 %copy-start.48 = (f32[64]{0:T(128)S(1)}, f32[64]{0:T(128)}, u32[]{:S(2)}) copy-start(f32[64]{0:T(128)} %copy-done.47) | copy-start | bytes 772
  281.3 18.4 %copy-start.54 = (f32[64]{0:T(128)S(1)}, f32[64]{0:T(128)}, u32[]{:S(2)}) copy-start(f32[64]{0:T(128)} %copy-done.53) | copy-start | bytes 772
  281.3 18.4 %copy-start.56 = (f32[64]{0:T(128)S(1)}, f32[64]{0:T(128)}, u32[]{:S(2)}) copy-start(f32[64]{0:T(128)} %copy-done.55) | copy-start | bytes 772
  281.3 20.1 %copy-start.2 = (bf16[1024,1024]{1,0:T(8,128)(2,1)S(1)}, bf16[1024,1024]{1,0:T(8,128)(2,1)}, u32[]{:S(2)}) copy-start(bf16[1024,1024]{1,0:T(8,128)(2,1)} %all-gather.4.cloned.1.call-done) | copy-start | bytes 6291460
  307.0 9.3 %copy-start.8 = (bf16[64,1024]{0,1:T(8,128)(2,1)S(1)}, bf16[64,1024]{0,1:T(8,128)(2,1)}, u32[]{:S(2)}) copy-start(bf16[64,1024]{0,1:T(8,128)(2,1)} %copy.66) | copy-start | bytes 393220
  359.4 9.0 %copy-start.19 = (bf16[64,2816]{1,0:T(8,128)(2,1)S(1)}, bf16[64,2816]{1,0:T(8,128)(2,1)}, u32[]{:S(2)}) copy-start(bf16[64,2816]{1,0:T(8,128)(2,1)} %copy-done.18) | copy-start | bytes 1081348
  359.5 494.2 %all-reduce.3.cloned.1.call-start = ((), (), s32[]{:S(2)}) async-start(), calls=%async_computation.7 | async-start | bytes 3211264 | tf_op jit(solution)/shard_map/psum | solution.py:199
  364.6 437.7 %copy-start.7 = (bf16[2,1,64,1024]{3,2,1,0:T(8,128)(2,1)S(1)}, bf16[2,1,64,1024]{3,2,1,0:T(8,128)(2,1)}, u32[]{:S(2)}) copy-start(bf16[2,1,64,1024]{3,2,1,0:T(8,128)(2,1)} %param.7) | copy-start | bytes 786436
  364.6 437.7 %copy-start.42 = (f32[64]{0:T(128)S(1)}, f32[64]{0:T(128)}, u32[]{:S(2)}) copy-start(f32[64]{0:T(128)} %copy-done.41) | copy-start | bytes 772
  364.6 437.7 %copy-start.44 = (f32[64]{0:T(128)S(1)}, f32[64]{0:T(128)}, u32[]{:S(2)}) copy-start(f32[64]{0:T(128)} %copy-done.43) | copy-start | bytes 772
  364.6 437.7 %copy-start.50 = (f32[64]{0:T(128)S(1)}, f32[64]{0:T(128)}, u32[]{:S(2)}) copy-start(f32[64]{0:T(128)} %copy-done.49) | copy-start | bytes 772
  364.6 437.7 %copy-start.52 = (f32[64]{0:T(128)S(1)}, f32[64]{0:T(128)}, u32[]{:S(2)}) copy-start(f32[64]{0:T(128)} %copy-done.51) | copy-start | bytes 772
  368.4 438.9 %copy-start.31 = (f32[64,1024]{1,0:T(8,128)S(1)}, f32[64,1024]{1,0:T(8,128)}, u32[]{:S(2)}) copy-start(f32[64,1024]{1,0:T(8,128)} %get-tuple-element.29) | copy-start | bytes 786436
  368.4 438.9 %copy-start.32 = (f32[64,1024]{1,0:T(8,128)S(1)}, f32[64,1024]{1,0:T(8,128)}, u32[]{:S(2)}) copy-start(f32[64,1024]{1,0:T(8,128)} %get-tuple-element.63) | copy-start | bytes 786436
  (30 other events, 157.2 us)
Sparse Core Ops, SparseCore 0:
  10.2 46.3 all-gather.3
  58.8 111.0 all-gather.5
  172.2 62.9 all-gather.7
  281.3 127.8 reduce-scatter.4
  414.0 383.3 reduce-scatter.2
  801.7 51.8 all-reduce.2
